TPU v7x, 256 devices: a whole 4x4x8 slice. The times are simulated.
256 devices in a mesh: req: 32 (over z, x), tp: 8 (over y, core).
Axes of the slice: x: 4, y: 4, z: 8, core: 2. Of those that a mesh axis runs over, the one named last changes fastest.
Arguments:
- hidden_in: bfloat16 [192, 64, 3072], P('req', None, 'tp'), may hold values from -3 to 3
- request_order: int32 [192], replicated, may hold values from 0 to 191, as said below
- norm_gain: bfloat16 [3072], replicated, may hold values from 0.099609375 to 1.8984375
- w_query: bfloat16 [3072, 3072], P(None, 'tp'), may hold values from -0.109375 to 0.109375
- key_weight: bfloat16 [3072, 1024], P(None, 'tp'), may hold values from -0.4375 to 0.4375
- value_weight: bfloat16 [3072, 1024], P(None, 'tp'), may hold values from -0.109375 to 0.109375
- w_out: bfloat16 [3072, 3072], P('tp'), may hold values from -0.109375 to 0.109375
- key_cache: bfloat16 [192, 8, 3456, 128], P('req', 'tp'), may hold values from -360 to 360
- cached_values: bfloat16 [192, 8, 3456, 128], P('req', 'tp'), may hold values from -24 to 24
- cache_lengths: int32 [192], P('req'), may hold values from 864 to 3456, as said below
- tree_parent: int32 [192, 64], P('req'), may hold values from 0 to 63, as said below
- kept_nodes: int32 [192, 8], P('req'), may hold values from 0 to 63
Outputs:
- layer_out: bfloat16 [192, 64, 3072], P('req', None, 'tp')
- appended: bfloat16 [192, 2, 8, 8, 128], P('req', None, None, 'tp')
Inputs may be any that keep to these rules, and one draw needn't show every extreme that they name: `request_order`: each request is held by exactly one slot. The 6 requests of one device's rows go to 6 different devices of req, and the slots of one device hold requests of 6 different devices. `cache_lengths`: some slot has exactly 3456 live positions. `tree_parent`: node 0 has parent 0; every other node's parent has a lower index.
All inputs are finite; a program needn't handle non-finite values.
Results may differ from a plain program's by a relative error of at most 0.0085.
The roundings to bfloat16 on the way count: a program that leaves them out, or rounds other values in their place, can miss the bound.
Values may be sent and summed in bfloat16 or wider, within the bound.
A program may use at most 128 MiB of HBM per device.

v0:
```python
import jax
import jax.numpy as jnp
from jax import lax
from jax.sharding import PartitionSpec as P

HEAD_WIDTH = 128
NORM_EPSILON = 1e-05


def rotary_embedding(vectors, token_positions):
    half_dim = vectors.shape[-1] // 2
    frequency = 500000.0 ** (-jnp.arange(half_dim, dtype=jnp.float32) * 2.0 / vectors.shape[-1])
    angles = token_positions[..., None] * frequency
    cosine = jnp.cos(angles)[..., None, :]
    sine = jnp.sin(angles)[..., None, :]
    first_half = vectors[..., :half_dim]
    second_half = vectors[..., half_dim:]
    return jnp.concatenate(
        [first_half * cosine - second_half * sine, second_half * cosine + first_half * sine],
        axis=-1,
    )


def body(
    hidden_in,
    request_order,
    norm_gain,
    w_query,
    key_weight,
    value_weight,
    w_out,
    key_cache,
    cached_values,
    cache_lengths,
    tree_parent,
    kept_nodes,
):
    slots_here = key_cache.shape[0]
    tree_length = hidden_in.shape[1]
    width_local = hidden_in.shape[2]
    local_groups = key_cache.shape[1]
    local_heads = w_query.shape[1] // HEAD_WIDTH
    group_width = local_heads // local_groups
    slot_ids = lax.axis_index("req") * slots_here + jnp.arange(slots_here, dtype=jnp.int32)
    own_order = request_order[slot_ids]
    piece = lax.all_gather(hidden_in, "req", axis=0, tiled=True)
    piece_ids = jnp.arange(piece.shape[0], dtype=jnp.int32)
    chooser = (own_order[:, None] == piece_ids[None, :]).astype(jnp.bfloat16)
    dealt = jnp.einsum("rm,mtd->rtd", chooser, piece, preferred_element_type=jnp.float32).astype(
        jnp.bfloat16
    )
    widened = lax.all_gather(dealt, "tp", axis=2, tiled=True).astype(jnp.float32)
    normalized_input = (
        widened
        * lax.rsqrt(jnp.mean(widened * widened, axis=-1, keepdims=True) + NORM_EPSILON)
        * norm_gain.astype(jnp.float32)
    ).astype(jnp.bfloat16)
    flat_rows = normalized_input.reshape(slots_here * tree_length, normalized_input.shape[2])
    query_rows = jnp.dot(flat_rows, w_query, preferred_element_type=jnp.float32).reshape(
        slots_here, tree_length, local_heads, HEAD_WIDTH
    )
    fresh_keys = jnp.dot(flat_rows, key_weight, preferred_element_type=jnp.float32).reshape(
        slots_here, tree_length, local_groups, HEAD_WIDTH
    )
    fresh_values = (
        jnp.dot(flat_rows, value_weight, preferred_element_type=jnp.float32)
        .astype(jnp.bfloat16)
        .reshape(slots_here, tree_length, local_groups, HEAD_WIDTH)
    )
    node_ids = jnp.arange(tree_length, dtype=jnp.int32)
    parent_link = (
        (tree_parent[:, :, None] == node_ids[None, None, :]) & (node_ids[None, :, None] > 0)
    ).astype(jnp.float32)
    ancestry = jnp.eye(tree_length, dtype=jnp.float32)[None] + parent_link
    for sweep in range(tree_length.bit_length()):
        ancestry = jnp.minimum(
            jnp.einsum("rij,rjk->rik", ancestry, ancestry, precision=lax.Precision.HIGHEST), 1.0
        )
    token_positions = cache_lengths.astype(jnp.float32)[:, None] + jnp.sum(ancestry, axis=-1) - 1.0
    rotated_query = (
        rotary_embedding(query_rows, token_positions)
        .astype(jnp.bfloat16)
        .reshape(slots_here, tree_length, local_groups, group_width, HEAD_WIDTH)
    )
    key_rot = rotary_embedding(fresh_keys, token_positions).astype(jnp.bfloat16)
    score_scale = HEAD_WIDTH ** (-0.5)
    cache_scores = (
        jnp.einsum(
            "rtgqd,rgcd->rgqtc", rotated_query, key_cache, preferred_element_type=jnp.float32
        )
        * score_scale
    )
    live_keys = jnp.arange(key_cache.shape[2], dtype=jnp.int32)[None, :] < cache_lengths[:, None]
    cache_scores = jnp.where(live_keys[:, None, None, None, :], cache_scores, -jnp.inf)
    tree_scores = (
        jnp.einsum("rtgqd,rsgd->rgqts", rotated_query, key_rot, preferred_element_type=jnp.float32)
        * score_scale
    )
    tree_scores = jnp.where(ancestry[:, None, None] > 0, tree_scores, -jnp.inf)
    row_max = jnp.maximum(jnp.max(cache_scores, axis=-1), jnp.max(tree_scores, axis=-1))
    cache_exp = jnp.exp(cache_scores - row_max[..., None])
    tree_exp = jnp.exp(tree_scores - row_max[..., None])
    row_total = jnp.sum(cache_exp, axis=-1) + jnp.sum(tree_exp, axis=-1)
    cache_weights = (cache_exp / row_total[..., None]).astype(jnp.bfloat16)
    tree_weights = (tree_exp / row_total[..., None]).astype(jnp.bfloat16)
    attended = jnp.einsum(
        "rgqtc,rgcd->rtgqd", cache_weights, cached_values, preferred_element_type=jnp.float32
    )
    attended = attended + jnp.einsum(
        "rgqts,rsgd->rtgqd", tree_weights, fresh_values, preferred_element_type=jnp.float32
    )
    attended = attended.astype(jnp.bfloat16).reshape(
        slots_here, tree_length, local_heads * HEAD_WIDTH
    )
    keep_select = (kept_nodes[:, :, None] == node_ids[None, None, :]).astype(jnp.bfloat16)
    stacked = jnp.stack([key_rot, fresh_values], axis=1)
    appended = jnp.einsum(
        "rkt,rxtgd->rxkgd", keep_select, stacked, preferred_element_type=jnp.float32
    ).astype(jnp.bfloat16)
    partials = jnp.dot(
        attended.reshape(-1, attended.shape[2]), w_out, preferred_element_type=jnp.float32
    )
    summed = lax.psum(partials, "tp")
    my_share = lax.dynamic_slice_in_dim(summed, lax.axis_index("tp") * width_local, width_local, 1)
    layer_out = (my_share.reshape(dealt.shape) + dealt.astype(jnp.float32)).astype(jnp.bfloat16)
    return (layer_out, appended)


def solution(mesh):
    placed = (
        P("req", None, "tp"),
        P(),
        P(),
        P(None, "tp"),
        P(None, "tp"),
        P(None, "tp"),
        P("tp", None),
        P("req", "tp", None, None),
        P("req", "tp", None, None),
        P("req"),
        P("req", None),
        P("req", None),
    )
    return jax.shard_map(
        body,
        mesh=mesh,
        in_specs=placed,
        out_specs=(P("req", None, "tp"), P("req", None, None, "tp", None)),
        check_vma=False,
    )
```

profile of v0, /device:TPU:2, one launch (start us, length us, event | category | flops | bytes accessed | tf_op | source)
XLA Modules:
  0.0 284.8 jit_solution(10960639715566622475)
XLA Ops:
  7.2 0.0 copy-start
  7.2 0.0 all-gather.3.cloned.1.call-start
  7.2 0.7 all-gather.3.cloned.1.call-update
  7.9 0.0 all-gather.5.cloned.1.call-start
  8.0 1.3 gather_fusion
  9.3 0.0 copy-start.3
  9.3 0.0 copy-start.5
  9.3 106.1 %all-gather.3.cloned.1.call-done = bf16[192,64,384]{2,1,0:T(8,128)(2,1)} async-done(((bf16[6,64,384]{2,1,0:T(8,128)(2,1)}), bf16[192,64,384]{2,1,0:T(8,128)(2,1)}) %all-gather.3.cloned.1.call-update) | async-done | bytes 9437200 | tf_op jit(solution)/shard_map/all_gather | solution.py:46
  115.4 11.9 %fusion.3 = bf16[6,64,384]{2,0,1:T(8,128)(2,1)S(1)} fusion(bf16[192,64,384]{2,1,0:T(8,128)(2,1)} %all-gather.3.cloned.1.call-done, s32[6]{0:T(128)S(1)} %gather_fusion), kind=kOutput, calls=%fused_computation.7 | convolution fusion | flops 56624256 | bytes 9732120 | tf_op jit(solution)/shard_map/rm,mtd->rtd/dot_general | solution.py:49
  127.3 0.8 copy.78
  128.1 0.0 all-gather.5.cloned.1.call-update
  128.1 0.0 all-reduce.2.cloned.1.call-start
  128.3 0.5 convolution_minimum_fusion.6
  128.7 0.3 convolution_minimum_fusion.5
  129.0 0.3 convolution_minimum_fusion.4
  129.4 0.3 convolution_minimum_fusion.3
  129.7 0.3 convolution_minimum_fusion.2
  130.0 0.3 convolution_minimum_fusion.1
  130.4 0.4 fusion.63
  130.8 0.1 copy.54
  131.0 4.5 %copy.51 = bf16[3072,384]{0,1:T(8,128)(2,1)} copy(bf16[3072,384]{1,0:T(8,128)(2,1)} %param.15) | data formatting | bytes 4718592 | tf_op args[3]
  135.5 0.1 add_add_fusion
  135.5 0.8 multiply_cosine_fusion.1
  136.3 0.1 iota_compare_fusion.1
  136.4 19.0 %all-gather.5.cloned.1.call-done = bf16[6,64,3072]{2,1,0:T(8,128)(2,1)} async-done(((bf16[6,64,384]{2,1,0:T(8,128)(2,1)}), bf16[6,64,3072]{2,1,0:T(8,128)(2,1)}) %all-gather.5.cloned.1.call-update) | async-done | bytes 2359312 | tf_op jit(solution)/shard_map/all_gather | solution.py:52
  155.4 2.4 fusion.11
  157.7 2.4 fusion.13
  160.2 0.0 slice-start
  160.2 0.8 convolution_bitcast_fusion
  161.0 0.8 fusion.38
  161.8 0.0 slice-start.1
  161.8 1.4 fusion.14
  163.2 0.3 subtract_convert_fusion
  163.6 6.9 %fusion.2 = (f32[6,3,64]{2,1,0:T(4,128)S(1)}, f32[6,64,3,3456]{3,1,2,0:T(8,128)}) fusion(pred[6,3456]{1,0:T(8,128)(4,1)S(1)} %iota_compare_fusion.1, bf16[6,1,3456,128]{3,2,1,0:T(8,128)(2,1)S(1)} %bitcast.146, bf16[6,64,3,64]{3,1,2,0:T(8,128)(2,1)S(1)} %get-tuple-element.11, bf16[6,64,3,64]{3,1,2,0:T(8,128)(2,1)S(1)} %get-tuple-element.10), kind=kOutput, calls=%fused_computation.6 | convolution fusion | flops 1031748480 | bytes 21553920 | tf_op jit(solution)/shard_map/rtgqd,rgcd->rgqtc/dot_general | solution.py:88
  170.5 0.4 fusion.64
  171.0 0.1 fusion.27
  171.1 9.2 %fusion.1 = f32[6,3,64]{2,1,0:T(4,128)S(1)} fusion(f32[6,64,3,3456]{3,1,2,0:T(8,128)} %get-tuple-element.19, f32[6,3,64]{2,1,0:T(4,128)S(1)} %max.9, pred[6,3456]{1,0:T(8,128)(4,1)S(1)} %iota_compare_fusion.1), kind=kLoop, calls=%fused_computation.5 | loop fusion | flops 15924096 | bytes 15955200 | tf_op jit(solution)/shard_map/reduce_sum | solution.py:103
  180.3 1.9 convolution_convert_fusion
  182.2 10.3 %fusion.17 = f32[6,128,3,64]{1,3,2,0:T(8,128)S(1)} fusion(bf16[6,1,3456,128]{3,2,1,0:T(8,128)(2,1)} %param.20, f32[6,3,64]{2,1,0:T(4,128)S(1)} %add.98, f32[6,3,64]{2,1,0:T(4,128)S(1)} %max.9, f32[6,64,3,3456]{3,1,2,0:T(8,128)} %get-tuple-element.19, pred[6,3456]{1,0:T(8,128)(4,1)S(1)} %iota_compare_fusion.1), kind=kOutput, calls=%fused_computation.25 | convolution fusion | flops 1039122432 | bytes 21853440 | tf_op jit(solution)/shard_map/rgqtc,rgcd->rtgqd/dot_general | solution.py:106
  192.5 0.3 fusion.24
  192.8 0.3 copy.56
  193.1 0.0 copy-start.6
  193.1 3.5 %fusion.28 = f32[384,3072]{1,0:T(8,128)} fusion(bf16[384,3072]{1,0:T(8,128)(2,1)S(1)} %copy-done, bf16[48,8,3,128]{3,2,1,0:T(4,128)(2,1)S(1)} %bitcast.149), kind=kOutput, calls=%fused_computation.48 | convolution fusion | flops 905969664 | bytes 7372800 | tf_op jit(solution)/shard_map/dot_general | solution.py:120
  196.7 0.0 all-reduce.2.cloned.1.call-update
  196.7 0.8 fusion.25
  197.5 78.8 %all-reduce.2.cloned.1.call-done = f32[384,3072]{1,0:T(8,128)} async-done(((f32[384,3072]{1,0:T(8,128)}), f32[384,3072]{1,0:T(8,128)}) %all-reduce.2.cloned.1.call-update) | async-done | bytes 4718608 | tf_op jit(solution)/shard_map/psum | solution.py:123
  276.3 1.1 constant_dynamic-slice_fusion
  277.4 0.8 add_convert_fusion
  (24 shorter events, 0.1 us)
Async XLA Ops:
  7.2 185.9 %copy-start = (bf16[384,3072]{1,0:T(8,128)(2,1)S(1)}, bf16[384,3072]{1,0:T(8,128)(2,1)}, u32[]{:S(2)}) copy-start(bf16[384,3072]{1,0:T(8,128)(2,1)} %param.18) | copy-start | bytes 7077892
  7.2 108.2 %all-gather.3.cloned.1.call-start = ((), (), s32[]{:S(2)}) async-start(), calls=%async_computation | async-start | bytes 9732096 | tf_op jit(solution)/shard_map/all_gather | solution.py:46
  7.9 147.5 %all-gather.5.cloned.1.call-start = ((), (), s32[]{:S(2)}) async-start(), calls=%async_computation.1 | async-start | bytes 2654208 | tf_op jit(solution)/shard_map/all_gather | solution.py:52
  9.3 118.9 %copy-start.4 = (s32[6]{0:T(128)S(1)}, s32[6]{0:T(128)}, u32[]{:S(2)}) copy-start(s32[6]{0:T(128)} %param.21) | copy-start | bytes 76
  9.3 118.9 %copy-start.3 = (bf16[3072]{0:T(1024)(128)(2,1)S(1)}, bf16[3072]{0:T(1024)(128)(2,1)}, u32[]{:S(2)}) copy-start(bf16[3072]{0:T(1024)(128)(2,1)} %param.14) | copy-start | bytes 18436
  9.3 118.9 %copy-start.5 = (s32[6,64]{1,0:T(8,128)S(1)}, s32[6,64]{1,0:T(8,128)}, u32[]{:S(2)}) copy-start(s32[6,64]{1,0:T(8,128)} %param.22) | copy-start | bytes 4612
  128.1 148.2 %all-reduce.2.cloned.1.call-start = ((), (), s32[]{:S(2)}) async-start(), calls=%async_computation.2 | async-start | bytes 9437184 | tf_op jit(solution)/shard_map/psum | solution.py:123
  155.4 4.8 %copy-start.2 = (bf16[3072,128]{1,0:T(8,128)(2,1)S(1)}, bf16[3072,128]{1,0:T(8,128)(2,1)}, u32[]{:S(2)}) copy-start(bf16[3072,128]{1,0:T(8,128)(2,1)} %param.16) | copy-start | bytes 2359300
  155.4 6.4 %copy-start.1 = (bf16[3072,384]{0,1:T(8,128)(2,1)S(1)}, bf16[3072,384]{0,1:T(8,128)(2,1)}, u32[]{:S(2)}) copy-start(bf16[3072,384]{0,1:T(8,128)(2,1)} %copy.51) | copy-start | bytes 7077892
  160.2 3.4 %slice-start = ((s8[5308416]{0:T(1024)(128)(4,1)}), s8[4194304]{0:T(1024)(128)(4,1)S(1)}, s32[]{:S(2)}) async-start(s8[5308416]{0:T(1024)(128)(4,1)} %bitcast.145), calls=%async_computation.3 | async-start | bytes 8388608
  161.8 1.7 slice-start.1
  193.1 3.6 %copy-start.6 = (s32[6,8]{1,0:T(8,128)S(1)}, s32[6,8]{1,0:T(8,128)}, u32[]{:S(2)}) copy-start(s32[6,8]{1,0:T(8,128)} %param.23) | copy-start | bytes 580
Sparse Core Ops, SparseCore 0:
  10.6 104.8 all-gather.2
  128.2 27.0 all-gather.4
  196.8 79.4 all-reduce.1
where the time goes:
time: 285 us
  waiting for transfers between devices  205 us (72%)
  matrix products  40.8 us (14%)
  other arithmetic  17 us (6%)
  between operations  14.1 us (5%)
  local copies, waits for them, and re-layouts  8.1 us (3%)
    all_gather x1, waiting for transfers between devices, body(): piece = lax.all_gather(hidden_in, 'req', axis=0, tiled=True)  106 us
    psum x1, waiting for transfers between devices, body(): summed = lax.psum(partials, 'tp')  78.8 us
    all_gather x1, waiting for transfers between devices, body(): lax.all_gather(dealt, 'tp', axis=2, tiled=True).astype(jnp.float32)  19 us
    dot_general x1, matrix products, body(): jnp.einsum('rm,mtd->rtd', chooser, piece, preferred_element_type=jnp.floa...  11.9 us
    dot_general x1, matrix products, body(): jnp.einsum('rgqtc,rgcd->rtgqd', cache_weights, cached_values, preferred_e...  10.3 us
    reduce_sum x2, other arithmetic, body(): row_total = jnp.sum(cache_exp, axis=-1) + jnp.sum(tree_exp, axis=-1)  9.32 us
    dot_general x1, matrix products, body(): jnp.einsum('rtgqd,rgcd->rgqtc', rotated_query, key_cache, preferred_eleme...  6.91 us
  transfers between devices with their start and end apart: 3, of which 3 were waited for; matrix products, arithmetic and copies ran while one was open for 4% of the time, Pallas kernels for 0%

commit v1 on v0

--- a/solution.py
+++ b/solution.py
@@ -43,7 +43,16 @@
     group_width = local_heads // local_groups
     slot_ids = lax.axis_index("req") * slots_here + jnp.arange(slots_here, dtype=jnp.int32)
     own_order = request_order[slot_ids]
-    piece = lax.all_gather(hidden_in, "req", axis=0, tiled=True)
+    recover_figure_over_axis = lambda original: jnp.concatenate(
+        lax.all_to_all(
+            jnp.stack([original] * lax.axis_size("req"), 0),
+            axis_name="req",
+            split_axis=0,
+            concat_axis=0,
+        ),
+        0,
+    )
+    piece = recover_figure_over_axis(hidden_in)
     piece_ids = jnp.arange(piece.shape[0], dtype=jnp.int32)
     chooser = (own_order[:, None] == piece_ids[None, :]).astype(jnp.bfloat16)
     dealt = jnp.einsum("rm,mtd->rtd", chooser, piece, preferred_element_type=jnp.float32).astype(

time: 285 us -> 418 us (1.47)
  waiting for transfers between devices: 205 us -> 321 us
  starting transfers between devices: 0.12 us -> 12.1 us
  local copies, waits for them, and re-layouts: 8.1 us -> 13.7 us
    all_to_all x0 -> x1, waiting for transfers between devices: none -> 212 us  [body(): lax.all_to_all(jnp.stack([original] * lax.axis_size('req'), 0), axis_name...]
    all_gather x1 -> x0, waiting for transfers between devices: 106 us -> none  [body(): piece = lax.all_gather(hidden_in, 'req', axis=0, tiled=True)]
    all_to_all x0 -> x1, starting transfers between devices: none -> 11.8 us  [body(): lax.all_to_all(jnp.stack([original] * lax.axis_size('req'), 0), axis_name...]
    all_gather x1, waiting for transfers between devices: 19 us -> 30.1 us  [body(): lax.all_gather(dealt, 'tp', axis=2, tiled=True).astype(jnp.float32)]
    another operation x0 -> x1, local copies, waits for them, and re-layouts: none -> 6.35 us  [body(): jnp.stack([original] * lax.axis_size('req'), 0)]
  transfers between devices with their start and end apart: 3 -> 3, of which waited for: 3 -> 3; matrix products, arithmetic and copies ran while one was open for 4% -> 2% of each run, Pallas kernels for 0% -> 0%
where the time goes in v1:
time: 418 us
  waiting for transfers between devices  321 us (77%)
  matrix products  39.6 us (9%)
  other arithmetic  17.1 us (4%)
  between operations  14.4 us (3%)
  local copies, waits for them, and re-layouts  13.7 us (3%)
  starting transfers between devices  12.1 us (3%)
    all_to_all x1, waiting for transfers between devices, body(): lax.all_to_all(jnp.stack([original] * lax.axis_size('req'), 0), axis_name...  212 us
    psum x1, waiting for transfers between devices, body(): summed = lax.psum(partials, 'tp')  78.8 us
    all_gather x1, waiting for transfers between devices, body(): lax.all_gather(dealt, 'tp', axis=2, tiled=True).astype(jnp.float32)  30.1 us
    dot_general x1, matrix products, body(): jnp.einsum('rm,mtd->rtd', chooser, piece, preferred_element_type=jnp.floa...  11.9 us
    all_to_all x1, starting transfers between devices, body(): lax.all_to_all(jnp.stack([original] * lax.axis_size('req'), 0), axis_name...  11.8 us
    dot_general x1, matrix products, body(): jnp.einsum('rgqtc,rgcd->rtgqd', cache_weights, cached_values, preferred_e...  10.2 us
    reduce_sum x2, other arithmetic, body(): row_total = jnp.sum(cache_exp, axis=-1) + jnp.sum(tree_exp, axis=-1)  9.32 us
  transfers between devices with their start and end apart: 3, of which 3 were waited for; matrix products, arithmetic and copies ran while one was open for 2% of the time, Pallas kernels for 0%

profile of v1, /device:TPU:2, one launch (start us, length us, event | category | flops | bytes accessed | tf_op | source)
XLA Modules:
  0.0 417.6 jit_solution(8316106347315133236)
XLA Ops:
  7.2 0.0 copy-start
  7.2 6.4 %stack.4 = bf16[32,6,64,384]{3,2,1,0:T(8,128)(2,1)} broadcast(bf16[6,64,384]{2,1,0:T(8,128)(2,1)} %param.12), dimensions={1,2,3} | broadcast | bytes 9732096 | tf_op jit(solution)/shard_map/stack | solution.py:48
  13.5 11.8 %all-to-all-start = ((bf16[32,6,64,384]{3,2,1,0:T(8,128)(2,1)}), bf16[32,6,64,384]{3,2,1,0:T(8,128)(2,1)}, u32[]{:S(2)}, u32[]{:S(2)}) async-start(bf16[32,6,64,384]{3,2,1,0:T(8,128)(2,1)} %stack.4), calls=%async_computation | async-start | bytes 18874368 | tf_op jit(solution)/shard_map/all_to_all | solution.py:47
  25.3 0.0 all-gather.2.cloned.1.call-start
  25.4 0.6 gather_fusion
  26.1 211.8 %all-to-all-done = bf16[32,6,64,384]{3,2,1,0:T(8,128)(2,1)} async-done(((bf16[32,6,64,384]{3,2,1,0:T(8,128)(2,1)}), bf16[32,6,64,384]{3,2,1,0:T(8,128)(2,1)}, u32[]{:S(2)}, u32[]{:S(2)}) %all-to-all-start) | async-done | bytes 9437216 | tf_op jit(solution)/shard_map/all_to_all | solution.py:47
  237.9 11.9 %fusion.3 = bf16[6,64,384]{2,0,1:T(8,128)(2,1)S(1)} fusion(bf16[192,64,384]{2,1,0:T(8,128)(2,1)} %bitcast.2, s32[6]{0:T(128)S(1)} %gather_fusion), kind=kOutput, calls=%fused_computation.7 | convolution fusion | flops 56624256 | bytes 9732120 | tf_op jit(solution)/shard_map/rm,mtd->rtd/dot_general | solution.py:58
  249.8 0.8 copy.64
  250.6 0.0 all-gather.2.cloned.1.call-update
  250.6 0.2 all-reduce.2.cloned.1.call-start
  250.9 4.3 %copy.37 = bf16[3072,384]{0,1:T(8,128)(2,1)} copy(bf16[3072,384]{1,0:T(8,128)(2,1)} %param.15) | data formatting | bytes 4718592 | tf_op args[3]
  255.2 0.5 convolution_minimum_fusion.6
  255.6 0.3 convolution_minimum_fusion.5
  256.0 0.3 convolution_minimum_fusion.4
  256.3 0.3 convolution_minimum_fusion.3
  256.6 0.3 convolution_minimum_fusion.2
  256.9 0.3 convolution_minimum_fusion.1
  257.3 0.4 fusion.63
  257.7 0.1 copy.40
  257.9 0.1 add_add_fusion
  258.0 0.8 multiply_cosine_fusion.1
  258.7 0.1 iota_compare_fusion.1
  258.8 30.1 %all-gather.2.cloned.1.call-done = bf16[6,64,3072]{2,1,0:T(8,128)(2,1)} async-done(((bf16[6,64,384]{2,1,0:T(8,128)(2,1)}), bf16[6,64,3072]{2,1,0:T(8,128)(2,1)}) %all-gather.2.cloned.1.call-update) | async-done | bytes 2359312 | tf_op jit(solution)/shard_map/all_gather | solution.py:61
  289.0 2.4 fusion.11
  291.3 2.5 fusion.13
  293.8 0.0 slice-start
  293.9 0.0 slice-start.1
  293.9 1.4 fusion.14
  295.3 0.8 convolution_bitcast_fusion
  296.1 0.8 fusion.38
  296.9 0.3 subtract_convert_fusion
  297.3 6.9 %fusion.2 = (f32[6,3,64]{2,1,0:T(4,128)S(1)}, f32[6,64,3,3456]{3,1,2,0:T(8,128)}) fusion(pred[6,3456]{1,0:T(8,128)(4,1)S(1)} %iota_compare_fusion.1, bf16[6,1,3456,128]{3,2,1,0:T(8,128)(2,1)S(1)} %bitcast.147, bf16[6,64,3,64]{3,1,2,0:T(8,128)(2,1)S(1)} %get-tuple-element.9, bf16[6,64,3,64]{3,1,2,0:T(8,128)(2,1)S(1)} %get-tuple-element.8), kind=kOutput, calls=%fused_computation.6 | convolution fusion | flops 1031748480 | bytes 21553920 | tf_op jit(solution)/shard_map/rtgqd,rgcd->rgqtc/dot_general | solution.py:97
  304.1 0.4 fusion.64
  304.6 0.1 fusion.27
  304.7 9.2 %fusion.1 = f32[6,3,64]{2,1,0:T(4,128)S(1)} fusion(f32[6,64,3,3456]{3,1,2,0:T(8,128)} %get-tuple-element.17, f32[6,3,64]{2,1,0:T(4,128)S(1)} %max.9, pred[6,3456]{1,0:T(8,128)(4,1)S(1)} %iota_compare_fusion.1), kind=kLoop, calls=%fused_computation.5 | loop fusion | flops 15924096 | bytes 15955200 | tf_op jit(solution)/shard_map/reduce_sum | solution.py:112
  313.9 0.0 copy-start.8
  314.0 10.2 %fusion.17 = f32[6,128,3,64]{1,3,2,0:T(8,128)S(1)} fusion(bf16[6,1,3456,128]{3,2,1,0:T(8,128)(2,1)} %param.20, f32[6,3,64]{2,1,0:T(4,128)S(1)} %add.98, f32[6,3,64]{2,1,0:T(4,128)S(1)} %max.9, f32[6,64,3,3456]{3,1,2,0:T(8,128)} %get-tuple-element.17, pred[6,3456]{1,0:T(8,128)(4,1)S(1)} %iota_compare_fusion.1), kind=kOutput, calls=%fused_computation.25 | convolution fusion | flops 1039122432 | bytes 21853440 | tf_op jit(solution)/shard_map/rgqtc,rgcd->rtgqd/dot_general | solution.py:115
  324.1 0.8 convolution_convert_fusion
  324.9 0.0 copy-start.11
  324.9 0.3 fusion.24
  325.3 0.3 copy.42
  325.5 0.1 copy-done.11
  325.6 3.6 fusion.28
  329.2 0.0 all-reduce.2.cloned.1.call-update
  329.2 0.8 fusion.25
  330.1 78.8 %all-reduce.2.cloned.1.call-done = f32[384,3072]{1,0:T(8,128)} async-done(((f32[384,3072]{1,0:T(8,128)}), f32[384,3072]{1,0:T(8,128)}) %all-reduce.2.cloned.1.call-update) | async-done | bytes 4718608 | tf_op jit(solution)/shard_map/psum | solution.py:132
  408.8 1.1 constant_dynamic-slice_fusion
  409.9 0.8 add_convert_fusion
  (36 shorter events, 0.1 us)
Async XLA Ops:
  7.2 318.4 %copy-start = (bf16[384,3072]{1,0:T(8,128)(2,1)S(1)}, bf16[384,3072]{1,0:T(8,128)(2,1)}, u32[]{:S(2)}) copy-start(bf16[384,3072]{1,0:T(8,128)(2,1)} %param.18) | copy-start | bytes 7077892
  13.5 11.9 %copy-start.1 = (s32[192]{0:T(256)S(1)}, s32[192]{0:T(256)}, u32[]{:S(2)}) copy-start(s32[192]{0:T(256)} %param.13) | copy-start | bytes 2308
  13.5 224.3 %all-to-all-start = ((bf16[32,6,64,384]{3,2,1,0:T(8,128)(2,1)}), bf16[32,6,64,384]{3,2,1,0:T(8,128)(2,1)}, u32[]{:S(2)}, u32[]{:S(2)}) async-start(bf16[32,6,64,384]{3,2,1,0:T(8,128)(2,1)} %stack.4), calls=%async_computation | async-start | bytes 18874368 | tf_op jit(solution)/shard_map/all_to_all | solution.py:47
  25.3 263.6 %all-gather.2.cloned.1.call-start = ((), (), s32[]{:S(2)}) async-start(), calls=%async_computation.1 | async-start | bytes 2654208 | tf_op jit(solution)/shard_map/all_gather | solution.py:61
  237.9 13.0 %copy-start.6 = (bf16[3072]{0:T(1024)(128)(2,1)S(1)}, bf16[3072]{0:T(1024)(128)(2,1)}, u32[]{:S(2)}) copy-start(bf16[3072]{0:T(1024)(128)(2,1)} %param.14) | copy-start | bytes 18436
  249.8 5.3 %copy-start.7 = (s32[6]{0:T(128)S(1)}, s32[6]{0:T(128)}, u32[]{:S(2)}) copy-start(s32[6]{0:T(128)} %param.21) | copy-start | bytes 76
  249.8 5.3 %copy-start.9 = (s32[6,64]{1,0:T(8,128)S(1)}, s32[6,64]{1,0:T(8,128)}, u32[]{:S(2)}) copy-start(s32[6,64]{1,0:T(8,128)} %param.22) | copy-start | bytes 4612
  250.6 158.2 %all-reduce.2.cloned.1.call-start = ((), (), s32[]{:S(2)}) async-start(), calls=%async_computation.2 | async-start | bytes 9437184 | tf_op jit(solution)/shard_map/psum | solution.py:132
  289.0 4.9 %copy-start.2 = (bf16[3072,384]{0,1:T(8,128)(2,1)S(1)}, bf16[3072,384]{0,1:T(8,128)(2,1)}, u32[]{:S(2)}) copy-start(bf16[3072,384]{0,1:T(8,128)(2,1)} %copy.37) | copy-start | bytes 7077892
  291.3 4.0 copy-start.3
  293.8 3.4 slice-start
  293.9 3.4 slice-start.1
  296.9 7.2 %copy-start.4 = (bf16[6,64,1,64]{3,1,0,2:T(8,128)(2,1)}, bf16[6,64,1,64]{3,1,0,2:T(8,128)(2,1)S(1)}, u32[]{:S(2)}) copy-start(bf16[6,64,1,64]{3,1,0,2:T(8,128)(2,1)S(1)} %get-tuple-element.11) | copy-start | bytes 147460
  313.9 10.2 %copy-start.8 = (bf16[3072,128]{1,0:T(8,128)(2,1)S(1)}, bf16[3072,128]{1,0:T(8,128)(2,1)}, u32[]{:S(2)}) copy-start(bf16[3072,128]{1,0:T(8,128)(2,1)} %param.17) | copy-start | bytes 2359300
  324.9 0.6 copy-start.11
  325.6 3.6 copy-start.5
  325.6 3.6 copy-start.10
  325.6 3.6 copy-start.12
Sparse Core Ops, SparseCore 0:
  250.7 38.1 all-gather.1
  329.3 79.4 all-reduce.1
